TPU v7x, 128 devices: a whole 4x4x4 slice. The times are simulated.
128 devices in a mesh: scen: 8 (over x, z_hi), border: 16 (over y, z_lo, core).
Axes of the slice: x: 4, y: 4, z: 4 (z_hi: 2, z_lo: 2; z = z_hi * 2 + z_lo), core: 2. Of those that a mesh axis runs over, the one named last changes fastest.
Arguments:
- border: bfloat16 [16, 512, 65536], P('scen', None, 'border'), may hold values from -1.5 to 1.5
- blocks: float32 [16, 512, 512], P('scen'), may hold values from -60 to 64, as said below
- root_diag: float32 [65536], P('border'), may hold values from 4 to 128
- live_rows: int32 [16], P('scen'), may hold values from 128 to 512, as said below
- panel_ids: int32 [4], replicated, may hold values from 0 to 255
Outputs:
- root_rows: float32 [16, 4096, 1024], P('border', 'scen')
- factor: float32 [4, 256, 256], replicated
Inputs may be any that keep to these rules, and one draw needn't show every extreme that they name: blocks[i] is a Gram matrix plus a positive diagonal of at least 1, hence symmetric positive definite. `live_rows`: each entry is a multiple of 128, and some scenario has 512.
All inputs are finite; a program needn't handle non-finite values.
Results may differ from a plain program's by a relative error of at most 0.0017.
Values may be sent and summed in bfloat16 or wider, within the bound.
No kernel may reach another device: no remote copies, remote signals or barrier semaphores. Data moves between devices by JAX's collectives and lax.ppermute only.
A program may use at most 128 MiB of HBM per device.

v0:
```python
import jax
import jax.numpy as jnp
from jax import lax
from jax.sharding import PartitionSpec as P

PW = 256
PANELS = 4


def broadcast(value, axis, source):
    kept = jnp.where(lax.axis_index(axis) == source, value, 0).astype(value.dtype)
    return lax.psum(kept, axis)


def on_device(border, blocks, root_diag, live_rows, panel_ids):
    scen_local, order, width = border.shape
    scen_count = lax.axis_size("scen")
    share = width // scen_count
    border_pos = lax.axis_index("border")
    scen_pos = lax.axis_index("scen")
    slabs = width // PW
    levels = jnp.arange(order, dtype=jnp.int32)
    keep = levels[None, :, None] >= (order - live_rows)[:, None, None]
    masked = jnp.where(keep, border, jnp.zeros_like(border))
    lower_factor = jnp.linalg.cholesky(blocks)
    identity = jnp.broadcast_to(jnp.eye(order, dtype=jnp.float32), blocks.shape)
    inverse = lax.linalg.triangular_solve(
        lower_factor, identity, left_side=True, lower=True
    ).astype(jnp.bfloat16)
    solved = jnp.einsum("ikr,irc->ikc", inverse, masked, preferred_element_type=jnp.float32).astype(
        jnp.bfloat16
    )
    panel_list = []
    for position in range(PANELS):
        chosen = panel_ids[position]
        owner = chosen // slabs
        offset = chosen % slabs * PW
        own_cols = lax.dynamic_slice_in_dim(solved, offset, PW, 2)
        panel_cols = broadcast(own_cols, "border", owner)
        panel_list.append(panel_cols)
    panels = jnp.concatenate(panel_list, axis=2)
    schur_cols = lax.psum_scatter(
        lax.dot_general(
            solved, panels, (((0, 1), (0, 1)), ((), ())), preferred_element_type=jnp.float32
        ),
        "scen",
        scatter_dimension=0,
        tiled=True,
    )
    base = border_pos * width + scen_pos * share
    global_cols = base + jnp.arange(share, dtype=jnp.int32)
    window_cols = (panel_ids[:, None] * PW + jnp.arange(PW, dtype=jnp.int32)[None, :]).reshape(-1)
    diag_part = lax.dynamic_slice_in_dim(root_diag, scen_pos * share, share)
    matches = global_cols[:, None] == window_cols[None, :]
    schur_cols = schur_cols + jnp.where(matches, diag_part[:, None], jnp.zeros((), jnp.float32))
    tiles = []
    for position in range(PANELS):
        local_start = panel_ids[position] * PW - base
        holds = (local_start >= 0) & (local_start < share)
        safe_start = jnp.clip(local_start, 0, share - PW)
        tile = lax.dynamic_slice(schur_cols, (safe_start, jnp.int32(position * PW)), (PW, PW))
        tiles.append(jnp.where(holds, tile, jnp.zeros_like(tile)))
    diag_block = lax.psum(jnp.stack(tiles), ("scen", "border"))
    factor = jnp.linalg.cholesky(diag_block)
    eye_stack = jnp.broadcast_to(jnp.eye(PW, dtype=jnp.float32), diag_block.shape)
    factor_inverse = lax.linalg.triangular_solve(factor, eye_stack, left_side=True, lower=True)
    shaped = schur_cols.reshape(share, PANELS, PW)
    solved_rows = jnp.einsum(
        "cpj,pkj->cpk", shaped, factor_inverse, precision=lax.Precision.HIGHEST
    )
    return (solved_rows.reshape(1, share, PANELS * PW), factor)


def solution(mesh):
    placed = (P("scen", None, "border"), P("scen", None, None), P("border"), P("scen"), P())
    return jax.shard_map(
        on_device,
        mesh=mesh,
        in_specs=placed,
        out_specs=(P("border", "scen", None), P()),
        check_vma=False,
    )
```

profile of v0, /device:TPU:1, one launch (start us, length us, event | category | flops | bytes accessed | tf_op | source)
XLA Modules:
  0.0 1063.2 jit_solution(11236807815509924732)
XLA Ops:
  7.8 0.8 iota_compare_fusion.1
  9.3 1.4 fusion.76
  20.5 3.0 copy.27
  23.6 2.1 fusion.14
  25.6 1.3 copy-done.1
  27.0 23.5 %custom-call.50 = f32[2,128,128]{2,1,0:T(8,128)S(1)} custom-call(f32[2,128,128]{2,1,0:T(8,128)S(1)} %cholesky.390), custom_call_target="Cholesky" | custom-call | tf_op jit(solution)/shard_map/jit(cholesky)/cholesky | solution.py:25
  50.5 19.7 %custom-call.51 = f32[2,1,128,128]{2,3,1,0:T(8,128)S(1)} custom-call(f32[2,1,128,128]{3,2,1,0:T(8,128)S(1)} %select_bitcast_fusion.7), custom_call_target="InvertDiagBlocksLowerTriangular" | custom-call | tf_op jit(solution)/shard_map/jit(cholesky)/cholesky | solution.py:25
  70.4 1.5 constant_dynamic-update-slice_fusion.5
  71.9 1.5 convolution_subtract_fusion.3
  73.4 0.7 cholesky.394
  74.1 24.9 %custom-call.52 = f32[2,128,128]{2,1,0:T(8,128)} custom-call(f32[2,128,128]{2,1,0:T(8,128)} %cholesky.394), custom_call_target="Cholesky" | custom-call | tf_op jit(solution)/shard_map/jit(cholesky)/cholesky | solution.py:25
  99.0 1.6 select_bitcast_fusion.6
  100.6 21.3 %custom-call.53 = f32[2,1,128,128]{2,3,1,0:T(8,128)} custom-call(f32[2,1,128,128]{3,2,1,0:T(8,128)} %get-tuple-element.72), custom_call_target="InvertDiagBlocksLowerTriangular" | custom-call | tf_op jit(solution)/shard_map/jit(cholesky)/cholesky | solution.py:25
  121.9 1.3 convolution_dynamic-update-slice_fusion
  123.2 1.6 convolution_subtract_fusion.5
  124.8 0.7 cholesky.399
  125.4 24.9 %custom-call.54 = f32[2,128,128]{2,1,0:T(8,128)} custom-call(f32[2,128,128]{2,1,0:T(8,128)} %cholesky.399), custom_call_target="Cholesky" | custom-call | tf_op jit(solution)/shard_map/jit(cholesky)/cholesky | solution.py:25
  150.3 1.6 select_bitcast_fusion.5
  151.9 21.1 %custom-call.55 = f32[2,1,128,128]{2,3,1,0:T(8,128)} custom-call(f32[2,1,128,128]{3,2,1,0:T(8,128)} %get-tuple-element.70), custom_call_target="InvertDiagBlocksLowerTriangular" | custom-call | tf_op jit(solution)/shard_map/jit(cholesky)/cholesky | solution.py:25
  173.0 1.2 convolution_dynamic-update-slice_fusion.1
  174.2 1.5 convolution_subtract_fusion.6
  175.7 23.9 %custom-call.56 = f32[2,128,128]{2,1,0:T(8,128)S(1)} custom-call(f32[2,128,128]{2,1,0:T(8,128)S(1)} %convolution_subtract_fusion.6), custom_call_target="Cholesky" | custom-call | tf_op jit(solution)/shard_map/jit(cholesky)/cholesky | solution.py:25
  199.6 1.0 select_reduce_fusion.4
  201.0 2.7 select_select_fusion
  203.6 14.1 %while.2 = (s32[]{:T(128)}, f32[2,512,512]{2,1,0:T(8,128)}, s32[4,2]{0,1:T(2,128)S(1)}, f32[4,2,128,128]{3,2,0,1:T(8,128)}, s32[]{:T(128)}) while((s32[]{:T(128)}, f32[2,512,512]{2,1,0:T(8,128)}, s32[4,2]{0,1:T(2,128)S(1)}, f32[4,2,128,128]{3,2,0,1:T(8,128)}, s32[]{:T(128)}) %tuple.68), condition=%wide.while_cond, body=%wide.while_body.sunk | while | flops 2 | bytes 263777 | solution.py:27
  204.2 2.9 bitcast_dynamic-update-slice_fusion.4
  207.8 2.9 bitcast_dynamic-update-slice_fusion.4
  211.3 2.9 bitcast_dynamic-update-slice_fusion.4
  214.9 2.9 bitcast_dynamic-update-slice_fusion.4
  217.7 79.4 %custom-call.57 = f32[2,4,128,128]{2,3,1,0:T(8,128)S(1)} custom-call(f32[2,4,128,128]{3,2,1,0:T(8,128)} %bitcast.125), custom_call_target="InvertDiagBlocksLowerTriangular" | custom-call | tf_op jit(solution)/shard_map/triangular_solve | solution.py:27
  297.9 1.5 convolution_subtract_fusion.2
  300.0 1.7 convolution_subtract_fusion
  302.4 2.1 fusion.21
  305.3 11.2 %fusion.3 = bf16[2,512,4096]{2,1,0:T(8,128)(2,1)} fusion(bf16[2,512,4096]{2,1,0:T(8,128)(2,1)} %param.5, pred[2,512]{1,0:T(4,128)(4,1)S(1)} %iota_compare_fusion.6, bf16[2,128,512]{2,1,0:T(8,128)(2,1)S(1)} %convolution_convert_fusion, bf16[2,128,512]{2,1,0:T(8,128)(2,1)S(1)} %get-tuple-element.80, bf16[2,128,512]{2,1,0:T(8,128)(2,1)S(1)} %get-tuple-element.82, ...), kind=kOutput, calls=%fused_computation.8 | convolution fusion | flops 4307550208 | bytes 17826816 | tf_op jit(solution)/shard_map/ikr,irc->ikc/dot_general | solution.py:30
  316.5 3.0 dynamic-slice_select_fusion.3
  319.6 127.5 %all-reduce.8.cloned.1.call-done = (bf16[2,512,256]{2,1,0:T(8,128)(2,1)}, bf16[2,512,256]{2,1,0:T(8,128)(2,1)}, bf16[2,512,256]{2,1,0:T(8,128)(2,1)}, bf16[2,512,256]{2,1,0:T(8,128)(2,1)}) async-done(((bf16[2,512,256]{2,1,0:T(8,128)(2,1)}, bf16[2,512,256]{2,1,0:T(8,128)(2,1)}, bf16[2,512,256]{2,1,0:T(8,128)(2,1)}, bf16[2,512,256]{2,1,0:T(8,128)(2,1)}), (bf16[2,512,256]{2,1,0:T(8,128)(2,1)}, ...) | async-done | bytes 2097168 | tf_op jit(solution)/shard_map/psum | solution.py:12
  447.1 15.2 %convolution_bitcast_fusion = f32[4096,1024]{0,1:T(8,128)} fusion(bf16[2,512,4096]{2,1,0:T(8,128)(2,1)} %fusion.3, bf16[2,512,256]{2,1,0:T(8,128)(2,1)} %get-tuple-element.44, bf16[2,512,256]{2,1,0:T(8,128)(2,1)} %get-tuple-element.45, bf16[2,512,256]{2,1,0:T(8,128)(2,1)} %get-tuple-element.46, bf16[2,512,256]{2,1,0:T(8,128)(2,1)} %get-tuple-element.47), kind=kOutput, calls=%fused_computation.4 | convolution fusion | flops 8598323200 | bytes 27262976 | tf_op jit(solution)/shard_map/dot_general | solution.py:43
  464.9 0.8 dynamic_slice.31
  465.7 189.8 %reduce-scatter.2.cloned.1.call-done = f32[512,1024]{0,1:T(8,128)} async-done(((f32[4096,1024]{0,1:T(8,128)}), f32[512,1024]{0,1:T(8,128)}) %reduce-scatter.2.cloned.1.call-update) | async-done | bytes 2097168 | tf_op jit(solution)/shard_map/reduce_scatter | solution.py:42
  655.5 1.9 select_add_fusion
  657.8 1.0 pad_maximum_fusion
  659.4 0.6 iota_compare_fusion.3
  660.1 0.7 fusion.75
  660.8 150.6 %all-reduce.6.cloned.1.call-done = f32[4,256,256]{1,2,0:T(8,128)} async-done(((f32[4,256,256]{1,2,0:T(8,128)}), f32[4,256,256]{1,2,0:T(8,128)}) %all-reduce.6.cloned.1.call-update) | async-done | bytes 1048592 | tf_op jit(solution)/shard_map/psum | solution.py:63
  811.3 2.6 copy.40
  814.0 1.4 fusion.38
  815.3 1.0 copy-done.4
  816.3 47.1 %custom-call.58 = f32[4,128,128]{2,1,0:T(8,128)S(1)} custom-call(f32[4,128,128]{2,1,0:T(8,128)S(1)} %cholesky.403), custom_call_target="Cholesky" | custom-call | tf_op jit(solution)/shard_map/jit(cholesky)/cholesky | solution.py:64
  863.5 0.7 select_bitcast_fusion
  864.2 40.7 %custom-call.59 = f32[4,1,128,128]{2,3,1,0:T(8,128)} custom-call(f32[4,1,128,128]{3,2,1,0:T(8,128)} %select_bitcast_fusion), custom_call_target="InvertDiagBlocksLowerTriangular" | custom-call | tf_op jit(solution)/shard_map/jit(cholesky)/cholesky | solution.py:64
  905.0 1.4 constant_dynamic-update-slice_fusion.1
  906.4 2.3 convolution_subtract_fusion.4
  908.7 48.4 %custom-call.60 = f32[4,128,128]{2,1,0:T(8,128)} custom-call(f32[4,128,128]{2,1,0:T(8,128)} %convolution_subtract_fusion.4), custom_call_target="Cholesky" | custom-call | tf_op jit(solution)/shard_map/jit(cholesky)/cholesky | solution.py:64
  957.1 1.0 select_reduce_fusion
  958.4 0.7 copy-done.3
  959.1 2.5 broadcast_select_fusion
  961.6 5.3 while.3
  962.2 2.0 bitcast_dynamic-update-slice_fusion.5
  964.8 2.0 bitcast_dynamic-update-slice_fusion.5
  966.9 80.3 %custom-call.61 = f32[4,2,128,128]{2,3,1,0:T(8,128)} custom-call(f32[4,2,128,128]{3,2,1,0:T(8,128)} %bitcast.126), custom_call_target="InvertDiagBlocksLowerTriangular" | custom-call | tf_op jit(solution)/shard_map/triangular_solve | solution.py:66
  1047.2 1.6 fusion.47
  1049.4 0.6 fusion.46
  1050.1 3.3 fusion.34
  1053.3 2.9 copy.46
  (75 shorter events, 10.5 us)
Async XLA Ops:
  7.2 439.9 %all-reduce.8.cloned.1.call-start = ((), (), s32[]{:S(2)}) async-start(), calls=%async_computation.3 | async-start | bytes 4194304 | tf_op jit(solution)/shard_map/psum | solution.py:12
  20.5 3.0 copy-start
  25.6 1.3 copy-start.1
  50.4 21.5 %copy-start.5 = (f32[2,128,128]{2,1,0:T(8,128)}, f32[2,128,128]{2,1,0:T(8,128)S(1)}, u32[]{:S(2)}) copy-start(f32[2,128,128]{2,1,0:T(8,128)S(1)} %custom-call.50) | copy-start | bytes 393220
  123.2 76.4 %copy-start.6 = (f32[2,128,128]{2,1,0:T(8,128)S(1)}, f32[2,128,128]{2,1,0:T(8,128)}, u32[]{:S(2)}) copy-start(f32[2,128,128]{2,1,0:T(8,128)} %copy-done.5) | copy-start | bytes 393220
  201.0 2.7 copy-start.11
  302.3 2.8 copy-start.10
  319.5 336.0 %reduce-scatter.2.cloned.1.call-start = ((), (), s32[]{:S(2)}) async-start(), calls=%async_computation.1 | async-start | bytes 18874368 | tf_op jit(solution)/shard_map/reduce_scatter | solution.py:42
  462.3 2.6 copy-start.9
  462.3 349.0 %all-reduce.6.cloned.1.call-start = ((), (), s32[]{:S(2)}) async-start(), calls=%async_computation.2 | async-start | bytes 2097152 | tf_op jit(solution)/shard_map/psum | solution.py:63
  811.3 2.6 copy-start.2
  815.3 1.0 copy-start.4
  908.7 52.8 %copy-start.12 = (s32[2]{0:T(128)S(1)}, s32[2]{0:T(128)}, u32[]{:S(2)}) copy-start(s32[2]{0:T(128)} %iota_multiply_fusion) | copy-start | bytes 28
  958.1 1.0 copy-start.3
  961.6 87.3 %copy-start.8 = (f32[128,256]{1,0:T(8,128)S(1)}, f32[128,256]{1,0:T(8,128)}, u32[]{:S(2)}) copy-start(f32[128,256]{1,0:T(8,128)} %get-tuple-element.66) | copy-start | bytes 393220
  1047.2 2.2 copy-start.7
Sparse Core Ops, SparseCore 0:
  319.7 127.3 all-reduce.7
  462.4 193.0 reduce-scatter.1
  660.9 150.3 all-reduce.5
where the time goes:
time: 1070 us; the launch traced here: 1060 us
  other arithmetic  480 us (45%)
  waiting for transfers between devices  468 us (44%)
  matrix products  52.6 us (5%)
  local copies, waits for them, and re-layouts  35.6 us (3%)
  between operations  26.9 us (3%)
    reduce_scatter x1, waiting for transfers between devices, on_device(): lax.psum_scatter(lax.dot_general(solved, panels, (((0, 1), (0, 1)), ((),...  190 us
    another operation x15, other arithmetic, on_device(): lower_factor = jnp.linalg.cholesky(blocks)  164 us
    psum x1, waiting for transfers between devices, on_device(): diag_block = lax.psum(jnp.stack(tiles), ('scen', 'border'))  151 us
    another operation x9, other arithmetic, on_device(): factor = jnp.linalg.cholesky(diag_block)  139 us
    psum x1, waiting for transfers between devices, broadcast(): return lax.psum(kept, axis)  128 us
    another operation x4, other arithmetic, on_device(): lax.linalg.triangular_solve(factor, eye_stack, left_side=True, lower=True)  84 us
    another operation x4, other arithmetic, on_device(): lax.linalg.triangular_solve(lower_factor, identity, left_side=True, lower...  83.4 us
  transfers between devices with their start and end apart: 3, of which 3 were waited for; matrix products, arithmetic and copies ran while one was open for 0% of the time, Pallas kernels for 0%

commit v1 on v0

--- a/solution.py
+++ b/solution.py
@@ -2,6 +2,7 @@
 import jax.numpy as jnp
 from jax import lax
 from jax.sharding import PartitionSpec as P
+from jax.lax import psum
 
 PW = 256
 PANELS = 4
@@ -60,7 +61,9 @@
         safe_start = jnp.clip(local_start, 0, share - PW)
         tile = lax.dynamic_slice(schur_cols, (safe_start, jnp.int32(position * PW)), (PW, PW))
         tiles.append(jnp.where(holds, tile, jnp.zeros_like(tile)))
-    diag_block = lax.psum(jnp.stack(tiles), ("scen", "border"))
+    diag_block = jnp.stack(tiles)
+    for k0 in ("border", "scen"):
+        diag_block = psum(diag_block, k0)
     factor = jnp.linalg.cholesky(diag_block)
     eye_stack = jnp.broadcast_to(jnp.eye(PW, dtype=jnp.float32), diag_block.shape)
     factor_inverse = lax.linalg.triangular_solve(factor, eye_stack, left_side=True, lower=True)

time: 1070 us -> 1140 us (1.065); the launches traced: 1060 us -> 1120 us
  waiting for transfers between devices: 468 us -> 525 us
    psum x1 -> x2, waiting for transfers between devices: 151 us -> 208 us  [on_device(): diag_block = psum(diag_block, k0)]
  transfers between devices with their start and end apart: 3 -> 4, of which waited for: 3 -> 4; matrix products, arithmetic and copies ran while one was open for 0% -> 0% of each run, Pallas kernels for 0% -> 0%
where the time goes in v1:
time: 1140 us; the launch traced here: 1120 us
  waiting for transfers between devices  525 us (46%)
  other arithmetic  480 us (42%)
  matrix products  52.6 us (5%)
  local copies, waits for them, and re-layouts  35.7 us (3%)
  between operations  26.9 us (2%)
    psum x2, waiting for transfers between devices, on_device(): diag_block = psum(diag_block, k0)  208 us
    reduce_scatter x1, waiting for transfers between devices, on_device(): lax.psum_scatter(lax.dot_general(solved, panels, (((0, 1), (0, 1)), ((),...  190 us
    another operation x15, other arithmetic, on_device(): lower_factor = jnp.linalg.cholesky(blocks)  164 us
    another operation x9, other arithmetic, on_device(): factor = jnp.linalg.cholesky(diag_block)  139 us
    psum x1, waiting for transfers between devices, broadcast(): return lax.psum(kept, axis)  128 us
    another operation x4, other arithmetic, on_device(): lax.linalg.triangular_solve(factor, eye_stack, left_side=True, lower=True)  83.9 us
    another operation x4, other arithmetic, on_device(): lax.linalg.triangular_solve(lower_factor, identity, left_side=True, lower...  83.4 us
  transfers between devices with their start and end apart: 4, of which 4 were waited for; matrix products, arithmetic and copies ran while one was open for 0% of the time, Pallas kernels for 0%

profile of v1, /device:TPU:1, one launch (start us, length us, event | category | flops | bytes accessed | tf_op | source)
XLA Modules:
  0.0 1120.2 jit_solution(14440775570741010069)
XLA Ops:
  7.8 0.8 iota_compare_fusion.1
  9.3 1.4 fusion.76
  20.5 3.0 copy.27
  23.6 2.1 fusion.14
  25.6 1.3 copy-done.1
  27.0 23.5 %custom-call.50 = f32[2,128,128]{2,1,0:T(8,128)S(1)} custom-call(f32[2,128,128]{2,1,0:T(8,128)S(1)} %cholesky.390), custom_call_target="Cholesky" | custom-call | tf_op jit(solution)/shard_map/jit(cholesky)/cholesky | solution.py:26
  50.5 19.7 %custom-call.51 = f32[2,1,128,128]{2,3,1,0:T(8,128)S(1)} custom-call(f32[2,1,128,128]{3,2,1,0:T(8,128)S(1)} %select_bitcast_fusion.7), custom_call_target="InvertDiagBlocksLowerTriangular" | custom-call | tf_op jit(solution)/shard_map/jit(cholesky)/cholesky | solution.py:26
  70.4 1.5 constant_dynamic-update-slice_fusion.5
  71.9 1.5 convolution_subtract_fusion.3
  73.4 0.7 cholesky.394
  74.1 24.9 %custom-call.52 = f32[2,128,128]{2,1,0:T(8,128)} custom-call(f32[2,128,128]{2,1,0:T(8,128)} %cholesky.394), custom_call_target="Cholesky" | custom-call | tf_op jit(solution)/shard_map/jit(cholesky)/cholesky | solution.py:26
  99.0 1.6 select_bitcast_fusion.6
  100.6 21.3 %custom-call.53 = f32[2,1,128,128]{2,3,1,0:T(8,128)} custom-call(f32[2,1,128,128]{3,2,1,0:T(8,128)} %get-tuple-element.72), custom_call_target="InvertDiagBlocksLowerTriangular" | custom-call | tf_op jit(solution)/shard_map/jit(cholesky)/cholesky | solution.py:26
  121.9 1.3 convolution_dynamic-update-slice_fusion
  123.2 1.6 convolution_subtract_fusion.5
  124.8 0.7 cholesky.399
  125.4 24.9 %custom-call.54 = f32[2,128,128]{2,1,0:T(8,128)} custom-call(f32[2,128,128]{2,1,0:T(8,128)} %cholesky.399), custom_call_target="Cholesky" | custom-call | tf_op jit(solution)/shard_map/jit(cholesky)/cholesky | solution.py:26
  150.3 1.6 select_bitcast_fusion.5
  151.9 21.1 %custom-call.55 = f32[2,1,128,128]{2,3,1,0:T(8,128)} custom-call(f32[2,1,128,128]{3,2,1,0:T(8,128)} %get-tuple-element.70), custom_call_target="InvertDiagBlocksLowerTriangular" | custom-call | tf_op jit(solution)/shard_map/jit(cholesky)/cholesky | solution.py:26
  173.0 1.2 convolution_dynamic-update-slice_fusion.1
  174.2 1.5 convolution_subtract_fusion.6
  175.7 23.9 %custom-call.56 = f32[2,128,128]{2,1,0:T(8,128)S(1)} custom-call(f32[2,128,128]{2,1,0:T(8,128)S(1)} %convolution_subtract_fusion.6), custom_call_target="Cholesky" | custom-call | tf_op jit(solution)/shard_map/jit(cholesky)/cholesky | solution.py:26
  199.6 1.0 select_reduce_fusion.4
  201.0 2.7 select_select_fusion
  203.6 14.1 %while.2 = (s32[]{:T(128)}, f32[2,512,512]{2,1,0:T(8,128)}, s32[4,2]{0,1:T(2,128)S(1)}, f32[4,2,128,128]{3,2,0,1:T(8,128)}, s32[]{:T(128)}) while((s32[]{:T(128)}, f32[2,512,512]{2,1,0:T(8,128)}, s32[4,2]{0,1:T(2,128)S(1)}, f32[4,2,128,128]{3,2,0,1:T(8,128)}, s32[]{:T(128)}) %tuple.68), condition=%wide.while_cond, body=%wide.while_body.sunk | while | flops 2 | bytes 263777 | solution.py:28
  204.2 2.9 bitcast_dynamic-update-slice_fusion.4
  207.8 2.9 bitcast_dynamic-update-slice_fusion.4
  211.3 2.9 bitcast_dynamic-update-slice_fusion.4
  214.9 2.9 bitcast_dynamic-update-slice_fusion.4
  217.7 79.4 %custom-call.57 = f32[2,4,128,128]{2,3,1,0:T(8,128)S(1)} custom-call(f32[2,4,128,128]{3,2,1,0:T(8,128)} %bitcast.125), custom_call_target="InvertDiagBlocksLowerTriangular" | custom-call | tf_op jit(solution)/shard_map/triangular_solve | solution.py:28
  297.9 1.5 convolution_subtract_fusion.2
  300.0 1.7 convolution_subtract_fusion
  302.4 2.1 fusion.21
  305.3 11.2 fusion.3
  316.5 3.0 dynamic-slice_select_fusion.3
  319.6 127.5 %all-reduce.11.cloned.1.call-done = (bf16[2,512,256]{2,1,0:T(8,128)(2,1)}, bf16[2,512,256]{2,1,0:T(8,128)(2,1)}, bf16[2,512,256]{2,1,0:T(8,128)(2,1)}, bf16[2,512,256]{2,1,0:T(8,128)(2,1)}) async-done(((bf16[2,512,256]{2,1,0:T(8,128)(2,1)}, bf16[2,512,256]{2,1,0:T(8,128)(2,1)}, bf16[2,512,256]{2,1,0:T(8,128)(2,1)}, bf16[2,512,256]{2,1,0:T(8,128)(2,1)}), (bf16[2,512,256]{2,1,0:T(8,128)(2,1)}, ...) | async-done | bytes 2097168 | tf_op jit(solution)/shard_map/psum | solution.py:13
  447.1 15.2 %convolution_bitcast_fusion = f32[4096,1024]{0,1:T(8,128)} fusion(bf16[2,512,4096]{2,1,0:T(8,128)(2,1)} %fusion.3, bf16[2,512,256]{2,1,0:T(8,128)(2,1)} %get-tuple-element.44, bf16[2,512,256]{2,1,0:T(8,128)(2,1)} %get-tuple-element.45, bf16[2,512,256]{2,1,0:T(8,128)(2,1)} %get-tuple-element.46, bf16[2,512,256]{2,1,0:T(8,128)(2,1)} %get-tuple-element.47), kind=kOutput, calls=%fused_computation.4 | convolution fusion | flops 8598323200 | bytes 27262976 | tf_op jit(solution)/shard_map/dot_general | solution.py:44
  464.9 0.8 dynamic_slice.31
  465.7 189.9 %reduce-scatter.2.cloned.1.call-done = f32[512,1024]{0,1:T(8,128)} async-done(((f32[4096,1024]{0,1:T(8,128)}), f32[512,1024]{0,1:T(8,128)}) %reduce-scatter.2.cloned.1.call-update) | async-done | bytes 2097168 | tf_op jit(solution)/shard_map/reduce_scatter | solution.py:43
  655.6 1.9 select_add_fusion
  657.8 1.0 pad_maximum_fusion
  658.9 122.8 %all-reduce.7.cloned.1.call-done = f32[4,256,256]{1,2,0:T(8,128)} async-done(((f32[4,256,256]{1,2,0:T(8,128)}), f32[4,256,256]{1,2,0:T(8,128)}) %all-reduce.7.cloned.1.call-update) | async-done | bytes 1048592 | tf_op jit(solution)/shard_map/psum | solution.py:66
  782.2 0.6 iota_compare_fusion.3
  782.9 0.7 fusion.75
  783.6 84.8 %all-reduce.9.cloned.1.call-done = f32[4,256,256]{1,2,0:T(8,128)} async-done(((f32[4,256,256]{1,2,0:T(8,128)}), f32[4,256,256]{1,2,0:T(8,128)}) %all-reduce.9.cloned.1.call-update) | async-done | bytes 1048592 | tf_op jit(solution)/shard_map/psum | solution.py:66
  868.4 2.6 copy.40
  871.0 1.4 fusion.38
  872.4 1.0 copy-done.4
  873.4 47.1 %custom-call.58 = f32[4,128,128]{2,1,0:T(8,128)S(1)} custom-call(f32[4,128,128]{2,1,0:T(8,128)S(1)} %cholesky.403), custom_call_target="Cholesky" | custom-call | tf_op jit(solution)/shard_map/jit(cholesky)/cholesky | solution.py:67
  920.6 0.7 select_bitcast_fusion
  921.3 40.7 %custom-call.59 = f32[4,1,128,128]{2,3,1,0:T(8,128)} custom-call(f32[4,1,128,128]{3,2,1,0:T(8,128)} %select_bitcast_fusion), custom_call_target="InvertDiagBlocksLowerTriangular" | custom-call | tf_op jit(solution)/shard_map/jit(cholesky)/cholesky | solution.py:67
  962.0 1.4 constant_dynamic-update-slice_fusion.1
  963.5 2.3 convolution_subtract_fusion.4
  965.8 48.4 %custom-call.60 = f32[4,128,128]{2,1,0:T(8,128)} custom-call(f32[4,128,128]{2,1,0:T(8,128)} %convolution_subtract_fusion.4), custom_call_target="Cholesky" | custom-call | tf_op jit(solution)/shard_map/jit(cholesky)/cholesky | solution.py:67
  1014.1 1.0 select_reduce_fusion
  1015.4 0.7 copy-done.3
  1016.1 2.5 broadcast_select_fusion
  1018.7 5.3 while.3
  1019.3 2.0 bitcast_dynamic-update-slice_fusion.5
  1021.9 2.0 bitcast_dynamic-update-slice_fusion.5
  1023.9 80.3 %custom-call.61 = f32[4,2,128,128]{2,3,1,0:T(8,128)} custom-call(f32[4,2,128,128]{3,2,1,0:T(8,128)} %bitcast.126), custom_call_target="InvertDiagBlocksLowerTriangular" | custom-call | tf_op jit(solution)/shard_map/triangular_solve | solution.py:69
  1104.2 1.6 fusion.47
  1107.1 3.3 fusion.34
  1110.4 2.9 copy.46
  (78 shorter events, 11.1 us)
Async XLA Ops:
  7.2 439.9 %all-reduce.11.cloned.1.call-start = ((), (), s32[]{:S(2)}) async-start(), calls=%async_computation.4 | async-start | bytes 4194304 | tf_op jit(solution)/shard_map/psum | solution.py:13
  20.5 3.0 copy-start
  25.6 1.3 copy-start.1
  50.4 21.5 %copy-start.5 = (f32[2,128,128]{2,1,0:T(8,128)}, f32[2,128,128]{2,1,0:T(8,128)S(1)}, u32[]{:S(2)}) copy-start(f32[2,128,128]{2,1,0:T(8,128)S(1)} %custom-call.50) | copy-start | bytes 393220
  123.2 76.4 %copy-start.6 = (f32[2,128,128]{2,1,0:T(8,128)S(1)}, f32[2,128,128]{2,1,0:T(8,128)}, u32[]{:S(2)}) copy-start(f32[2,128,128]{2,1,0:T(8,128)} %copy-done.5) | copy-start | bytes 393220
  201.0 2.7 copy-start.11
  302.3 2.8 copy-start.10
  319.5 336.0 %reduce-scatter.2.cloned.1.call-start = ((), (), s32[]{:S(2)}) async-start(), calls=%async_computation.1 | async-start | bytes 18874368 | tf_op jit(solution)/shard_map/reduce_scatter | solution.py:43
  462.3 2.6 copy-start.9
  462.3 319.4 %all-reduce.7.cloned.1.call-start = ((), (), s32[]{:S(2)}) async-start(), calls=%async_computation.2 | async-start | bytes 2097152 | tf_op jit(solution)/shard_map/psum | solution.py:66
  658.9 209.5 %all-reduce.9.cloned.1.call-start = ((), (), s32[]{:S(2)}) async-start(), calls=%async_computation.3 | async-start | bytes 2097152 | tf_op jit(solution)/shard_map/psum | solution.py:66
  868.4 2.6 copy-start.2
  872.4 1.0 copy-start.4
  965.8 52.8 %copy-start.12 = (s32[2]{0:T(128)S(1)}, s32[2]{0:T(128)}, u32[]{:S(2)}) copy-start(s32[2]{0:T(128)} %iota_multiply_fusion) | copy-start | bytes 28
  1015.1 1.0 copy-start.3
  1018.6 87.3 %copy-start.8 = (f32[128,256]{1,0:T(8,128)S(1)}, f32[128,256]{1,0:T(8,128)}, u32[]{:S(2)}) copy-start(f32[128,256]{1,0:T(8,128)} %get-tuple-element.66) | copy-start | bytes 393220
  1104.2 2.2 copy-start.7
Sparse Core Ops, SparseCore 0:
  319.7 127.3 all-reduce.10
  462.4 193.0 reduce-scatter.1
  659.0 122.6 all-reduce.6
  784.1 84.2 all-reduce.8
